TPU v7x, 256 devices: a whole 4x4x8 slice. The times are simulated.
256 devices in a mesh: seq: 32 (over z, y), head: 8 (over x, core).
Axes of the slice: x: 4, y: 4, z: 8, core: 2. Of those that a mesh axis runs over, the one named last changes fastest.
Arguments:
- hidden_states: bfloat16 [8, 5, 8192], P(None, None, 'seq'), may hold values from -6 to 6
- w_query: bfloat16 [8192, 8192], P('seq', 'head'), may hold values from -0.0625 to 0.0625
- w_key: bfloat16 [8192, 1024], P('seq', 'head'), may hold values from -0.15625 to 0.15625
- w_value: bfloat16 [8192, 1024], P('seq', 'head'), may hold values from -0.0625 to 0.0625
- w_out: bfloat16 [8192, 8192], P('head', 'seq'), may hold values from -0.0625 to 0.0625
- key_cache: bfloat16 [8, 32768, 1024], P(None, 'seq', 'head'), may hold values from -104 to 104
- value_cache: bfloat16 [8, 32768, 1024], P(None, 'seq', 'head'), may hold values from -6 to 6
- context_lengths: int32 [8], replicated, may hold values from 8192 to 32768, as said below
- keep_blocks: int32 [8, 256], P(None, 'seq'), may hold values from 0 to 1, as said below
Outputs:
- verify_out: bfloat16 [8, 5, 8192], P(None, None, 'seq')
- draft_out: bfloat16 [8, 4, 8192], P(None, None, 'seq')
Inputs may be any that keep to these rules, and one draw needn't show every extreme that they name: `keep_blocks`: block 0 of every sequence is kept. `context_lengths`: one sequence has length 32768.
All inputs are finite; a program needn't handle non-finite values.
Results may differ from a plain program's by a relative error of at most 0.017.
Values may be sent and summed in bfloat16 or wider, within the bound.
No kernel may reach another device: no remote copies, remote signals or barrier semaphores. Data moves between devices by JAX's collectives and lax.ppermute only.
A program may use at most 64 MiB of HBM per device.

v0:
```python
import jax
import jax.numpy as jnp
from jax import lax
from jax.sharding import PartitionSpec as P

HEAD_DIM = 128
BLOCK = 128
big_negative = -1e30


def rotate(values_in, positions):
    half_dim = HEAD_DIM // 2
    inverse = 500000.0 ** (-(jnp.arange(half_dim, dtype=jnp.float32) * 2.0) / HEAD_DIM)
    angles = positions[:, :, None, None].astype(jnp.float32) * inverse
    cosine = jnp.cos(angles)
    sine = jnp.sin(angles)
    first_half = values_in[..., :half_dim]
    second_half = values_in[..., half_dim:]
    return jnp.concatenate(
        [first_half * cosine - second_half * sine, second_half * cosine + first_half * sine],
        axis=-1,
    )


def partial_softmax(scores, mask_full, cache_values):
    masked = jnp.where(mask_full, scores, big_negative)
    peak_value = jnp.max(masked, axis=-1)
    weights = jnp.where(mask_full, jnp.exp(masked - peak_value[..., None]), 0.0)
    weighted = jnp.einsum(
        "bkjgt,btkd->bkjgd",
        weights.astype(jnp.bfloat16),
        cache_values,
        preferred_element_type=jnp.float32,
    )
    return (peak_value, jnp.sum(weights, axis=-1), weighted)


def finish(partials, new_scores, causal, new_values):
    peak_cache, total_sum, weighted = partials
    mask_full = causal[None, None, :, None, :]
    masked = jnp.where(mask_full, new_scores, big_negative)
    peak_value = jnp.maximum(peak_cache, jnp.max(masked, axis=-1))
    factor_old = jnp.exp(peak_cache - peak_value)
    weights = jnp.where(mask_full, jnp.exp(masked - peak_value[..., None]), 0.0)
    total_sum = total_sum * factor_old + jnp.sum(weights, axis=-1)
    weighted = weighted * factor_old[..., None] + jnp.einsum(
        "bkjgi,bikd->bkjgd",
        weights.astype(jnp.bfloat16),
        new_values,
        preferred_element_type=jnp.float32,
    )
    result = weighted / total_sum[..., None]
    batch_size, kv_local, positions_count, group_size, head_size = result.shape
    return result.transpose(0, 2, 1, 3, 4).reshape(
        batch_size * positions_count, kv_local * group_size * head_size
    )


def per_device(
    hidden_states,
    w_query,
    w_key,
    w_value,
    w_out,
    key_cache,
    value_cache,
    context_lengths,
    keep_blocks,
):
    seq_index = lax.axis_index("seq")
    batch_size, verify, width_local = hidden_states.shape
    draft_len = verify - 1
    kv_local = key_cache.shape[2] // HEAD_DIM
    heads_local = w_query.shape[1] // HEAD_DIM
    group_size = heads_local // kv_local
    ctx_local = key_cache.shape[1]
    score_scale = HEAD_DIM ** (-0.5)
    tok_rows = hidden_states.reshape(batch_size * verify, width_local)
    query_part = jnp.dot(tok_rows, w_query, preferred_element_type=jnp.float32)
    key_part = jnp.dot(tok_rows, w_key, preferred_element_type=jnp.float32)
    value_part = jnp.dot(tok_rows, w_value, preferred_element_type=jnp.float32)
    query_sum, key_sum, value_sum = lax.psum((query_part, key_part, value_part), "seq")
    positions = context_lengths[:, None] + jnp.arange(verify, dtype=jnp.int32)[None, :]
    query_rot = rotate(
        query_sum.reshape(batch_size, verify, heads_local, HEAD_DIM), positions
    ).astype(jnp.bfloat16)
    new_key = rotate(key_sum.reshape(batch_size, verify, kv_local, HEAD_DIM), positions).astype(
        jnp.bfloat16
    )
    new_values = value_sum.reshape(batch_size, verify, kv_local, HEAD_DIM).astype(jnp.bfloat16)
    grouped = query_rot.reshape(batch_size, verify, kv_local, group_size, HEAD_DIM)
    cache_keys = key_cache.reshape(batch_size, ctx_local, kv_local, HEAD_DIM)
    cache_values = value_cache.reshape(batch_size, ctx_local, kv_local, HEAD_DIM)
    scores = (
        jnp.einsum("bjkgd,btkd->bkjgt", grouped, cache_keys, preferred_element_type=jnp.float32)
        * score_scale
    )
    key_positions = seq_index * ctx_local + jnp.arange(ctx_local, dtype=jnp.int32)
    live_mask = key_positions[None, :] < context_lengths[:, None]
    kept_mask = live_mask & (jnp.repeat(keep_blocks, BLOCK, axis=1) > 0)
    target_peak, target_total, target_weighted = partial_softmax(
        scores, live_mask[:, None, None, None, :], cache_values
    )
    draft_peak, draft_total, draft_weighted = partial_softmax(
        scores[:, :, :draft_len], kept_mask[:, None, None, None, :], cache_values
    )
    peak_target, peak_draft = lax.pmax((target_peak, draft_peak), "seq")
    factor_target = jnp.exp(target_peak - peak_target)
    factor_draft = jnp.exp(draft_peak - peak_draft)
    sum_parts = lax.psum(
        (
            target_total * factor_target,
            target_weighted * factor_target[..., None],
            draft_total * factor_draft,
            draft_weighted * factor_draft[..., None],
        ),
        "seq",
    )
    merged = (peak_target, sum_parts[0], sum_parts[1], peak_draft, sum_parts[2], sum_parts[3])
    causal = jnp.arange(verify)[None, :] <= jnp.arange(verify)[:, None]
    new_scores = (
        jnp.einsum("bjkgd,bikd->bkjgi", grouped, new_key, preferred_element_type=jnp.float32)
        * score_scale
    )
    target_heads = finish(merged[0:3], new_scores, causal, new_values)
    draft_heads = finish(merged[3:6], new_scores[:, :, :draft_len], causal[:draft_len], new_values)
    attended = jnp.concatenate([target_heads, draft_heads], axis=0).astype(jnp.bfloat16)
    projected = jnp.dot(attended, w_out, preferred_element_type=jnp.float32)
    summed = lax.psum(projected.astype(jnp.bfloat16), "head")
    verify_out = summed[: batch_size * verify].reshape(batch_size, verify, summed.shape[1])
    draft_out = summed[batch_size * verify :].reshape(batch_size, draft_len, summed.shape[1])
    return (verify_out, draft_out)


def solution(mesh):
    placed = (
        P(None, None, "seq"),
        P("seq", "head"),
        P("seq", "head"),
        P("seq", "head"),
        P("head", "seq"),
        P(None, "seq", "head"),
        P(None, "seq", "head"),
        P(),
        P(None, "seq"),
    )
    return jax.shard_map(
        per_device,
        mesh=mesh,
        in_specs=placed,
        out_specs=(P(None, None, "seq"), P(None, None, "seq")),
        check_vma=False,
    )
```

profile of v0, /device:TPU:32, one launch (start us, length us, event | category | flops | bytes accessed | tf_op | source)
XLA Modules:
  0.0 634.3 jit_solution(9448252033808468446)
XLA Ops:
  7.3 0.9 copy.42
  8.2 1.2 convolution_bitcast_fusion
  12.8 144.7 %all-reduce.6.cloned.1.call-done = f32[8,5,8,128]{3,2,1,0:T(8,128)} async-done(((f32[8,5,8,128]{3,2,1,0:T(8,128)}), f32[8,5,8,128]{3,2,1,0:T(8,128)}) %all-reduce.6.cloned.1.call-update) | async-done | bytes 163856 | tf_op jit(solution)/shard_map/psum | solution.py:82
  157.5 1.1 subtract_convert_fusion
  158.7 0.9 select_reduce_fusion
  159.6 1.0 fusion.27
  160.9 1.0 fusion.30
  161.9 134.7 %all-reduce.2 = (f32[8,1,4,8]{3,2,0,1:T(4,128)}, f32[8,1,5,8]{3,2,0,1:T(8,128)S(1)}) all-reduce(f32[8,1,4,8]{3,2,0,1:T(4,128)} %bitcast.153, f32[8,1,5,8]{3,2,0,1:T(8,128)S(1)} %bitcast.151), channel_id=1, replica_groups=mesh['seq'=32,'head'=8] {'seq'}, use_global_device_ids=true, to_apply=%region_11.12 | all-reduce | flops 576 | bytes 4608 | tf_op jit(solution)/shard_map/pmax | solution.py:107
  296.6 1.4 bitcast_multiply_fusion
  298.0 1.4 bitcast_multiply_fusion.1
  299.4 138.9 %all-reduce = (f32[8,5,1,128]{3,1,0,2:T(8,128)}, f32[8,1,4,8]{3,2,0,1:T(4,128)}, bf16[40,128]{1,0:T(8,128)(2,1)}, f32[8,1,5,8]{3,2,0,1:T(8,128)}) all-reduce(f32[8,5,1,128]{3,1,0,2:T(8,128)} %reshape.256, f32[8,1,4,8]{3,2,0,1:T(4,128)} %get-tuple-element.35, f32[40,128]{1,0:T(8,128)} %fusion.88, ...), channel_id=1, replica_groups=mesh['seq'=32,'head'=8] {'seq'}, use_global_device_ids=true, to_apply=%region_4.5 | all-reduce | flops 10816 | bytes 76288 | tf_op jit(solution)/shard_map/psum | solution.py:82
  438.2 1.0 fusion.73
  439.3 1.4 fusion.66
  440.6 0.8 select_reduce_fusion.1
  442.0 2.0 fusion.47
  444.0 3.0 fusion.12
  447.1 1.2 fusion.20
  449.8 0.8 fusion.51
  450.6 0.8 fusion.78
  451.5 0.8 fusion.74
  452.3 147.3 %all-reduce.8.cloned.1.call-done = (f32[8,1,4,8,128]{4,3,2,0,1:T(8,128)}, f32[8,1,5,8,128]{4,3,2,0,1:T(8,128)}) async-done(((f32[8,1,4,8,128]{4,3,2,0,1:T(8,128)}, f32[8,1,5,8,128]{4,3,2,0,1:T(8,128)}), (f32[8,1,4,8,128]{4,3,2,0,1:T(8,128)}, f32[8,1,5,8,128]{4,3,2,0,1:T(8,128)})) %all-reduce.8.cloned.1.call-update) | async-done | bytes 294928 | tf_op jit(solution)/shard_map/psum | solution.py:110
  599.6 1.2 fusion.23
  600.9 1.1 fusion.26
  602.2 23.9 %psum.63 = bf16[72,256]{1,0:T(8,128)(2,1)S(1)} all-reduce(bf16[72,256]{1,0:T(8,128)(2,1)S(1)} %convolution_convert_fusion), channel_id=1, replica_groups=mesh['seq'=32,'head'=8] {'head'}, use_global_device_ids=true, to_apply=%region_17.18 | all-reduce | flops 18432 | bytes 73728 | tf_op jit(solution)/shard_map/psum | solution.py:129
  (75 shorter events, 7.2 us)
Async XLA Ops:
  7.2 151.5 %copy-start = (bf16[8,1024,128]{2,1,0:T(8,128)(2,1)S(1)}, bf16[8,1024,128]{2,1,0:T(8,128)(2,1)}, u32[]{:S(2)}) copy-start(bf16[8,1024,128]{2,1,0:T(8,128)(2,1)} %param.14) | copy-start | bytes 6291460
  7.2 3.1 copy-start.19
  7.2 3.1 copy-start.17
  7.2 3.2 copy-start.11
  7.2 4.0 copy-start.12
  7.2 150.3 %all-reduce.6.cloned.1.call-start = ((), (), s32[]{:S(2)}) async-start(), calls=%async_computation | async-start | bytes 327680 | tf_op jit(solution)/shard_map/psum | solution.py:82
  10.1 589.5 %all-reduce.8.cloned.1.call-start = ((), (), s32[]{:S(2)}) async-start(), calls=%async_computation.1 | async-start | bytes 589824 | tf_op jit(solution)/shard_map/psum | solution.py:110
  10.2 148.5 %copy-start.18 = (f32[64]{0:T(128)}, f32[64]{0:T(128)S(1)}, u32[]{:S(2)}) copy-start(f32[64]{0:T(128)S(1)} %multiply_power_fusion) | copy-start | bytes 772
  10.2 1.7 copy-start.16
  10.3 148.4 %copy-start.13 = (f32[8,5]{1,0:T(8,128)}, f32[8,5]{1,0:T(8,128)S(1)}, u32[]{:S(2)}) copy-start(f32[8,5]{1,0:T(8,128)S(1)} %add_convert_fusion.1) | copy-start | bytes 484
  12.8 146.8 %copy-start.10 = (pred[8,1024]{1,0:T(8,128)(4,1)}, pred[8,1024]{1,0:T(8,128)(4,1)S(1)}, u32[]{:S(2)}) copy-start(pred[8,1024]{1,0:T(8,128)(4,1)S(1)} %get-tuple-element.37) | copy-start | bytes 24580
  12.8 148.0 %copy-start.8 = (pred[8,1024]{1,0:T(8,128)(4,1)}, pred[8,1024]{1,0:T(8,128)(4,1)S(1)}, u32[]{:S(2)}) copy-start(pred[8,1024]{1,0:T(8,128)(4,1)S(1)} %get-tuple-element.38) | copy-start | bytes 24580
  158.7 1.0 copy-start.1
  160.9 1.0 copy-start.5
  296.6 144.9 %copy-start.3 = (f32[8,1,5,8]{3,2,0,1:T(8,128)}, f32[8,1,5,8]{3,2,0,1:T(8,128)S(1)}, u32[]{:S(2)}) copy-start(f32[8,1,5,8]{3,2,0,1:T(8,128)S(1)} %get-tuple-element.19) | copy-start | bytes 3844
  441.4 0.6 copy-start.7
  444.0 3.0 copy-start.6
  444.0 3.0 copy-start.9
  444.0 3.0 copy-start.14
  444.0 3.0 copy-start.20
  447.0 4.4 copy-start.15
  447.0 4.4 copy-start.4
  450.6 151.4 %copy-start.2 = (bf16[1024,256]{1,0:T(8,128)(2,1)S(1)}, bf16[1024,256]{1,0:T(8,128)(2,1)}, u32[]{:S(2)}) copy-start(bf16[1024,256]{1,0:T(8,128)(2,1)} %param.13) | copy-start | bytes 1572868
Sparse Core Ops, SparseCore 0:
  11.5 146.0 all-reduce.5
  450.7 148.8 all-reduce.7
where the time goes:
time: 635 us; the launch traced here: 634 us
  blocking collectives  298 us (47%)
  waiting for transfers between devices  292 us (46%)
  between operations  14.4 us (2%)
  other arithmetic  14.2 us (2%)
  matrix products  11.2 us (2%)
    psum x1, waiting for transfers between devices, per_device(): lax.psum((target_total * factor_target, target_weighted * factor_target[....  147 us
    psum x1, waiting for transfers between devices, per_device(): lax.psum((query_part, key_part, value_part), 'seq')  145 us
    psum x1, blocking collectives, per_device(): lax.psum((query_part, key_part, value_part), 'seq')  139 us
    pmax x1, blocking collectives, per_device(): peak_target, peak_draft = lax.pmax((target_peak, draft_peak), 'seq')  135 us
    psum x1, blocking collectives, per_device(): summed = lax.psum(projected.astype(jnp.bfloat16), 'head')  23.9 us
  transfers between devices with their start and end apart: 2, of which 2 were waited for; matrix products, arithmetic and copies ran while one was open for 1% of the time, Pallas kernels for 0%

commit v1 on v0

--- a/solution.py
+++ b/solution.py
@@ -126,7 +126,7 @@
     draft_heads = finish(merged[3:6], new_scores[:, :, :draft_len], causal[:draft_len], new_values)
     attended = jnp.concatenate([target_heads, draft_heads], axis=0).astype(jnp.bfloat16)
     projected = jnp.dot(attended, w_out, preferred_element_type=jnp.float32)
-    summed = lax.psum(projected.astype(jnp.bfloat16), "head")
+    summed = jnp.sum(lax.all_gather(projected.astype(jnp.bfloat16), "head"), axis=0)
     verify_out = summed[: batch_size * verify].reshape(batch_size, verify, summed.shape[1])
     draft_out = summed[batch_size * verify :].reshape(batch_size, draft_len, summed.shape[1])
     return (verify_out, draft_out)

time: 635 us -> 627 us (0.987)
  blocking collectives: 298 us -> 287 us
    psum x1 -> x0, blocking collectives: 23.9 us -> none  [per_device(): summed = lax.psum(projected.astype(jnp.bfloat16), 'head')]
    all_gather x0 -> x1, blocking collectives: none -> 13.2 us  [per_device(): lax.all_gather(projected.astype(jnp.bfloat16), 'head')]
where the time goes in v1:
time: 627 us; the launch traced here: 624 us
  waiting for transfers between devices  292 us (47%)
  blocking collectives  287 us (46%)
  between operations  14.4 us (2%)
  other arithmetic  14.2 us (2%)
  matrix products  11.2 us (2%)
    psum x1, waiting for transfers between devices, per_device(): lax.psum((target_total * factor_target, target_weighted * factor_target[....  147 us
    psum x1, waiting for transfers between devices, per_device(): lax.psum((query_part, key_part, value_part), 'seq')  145 us
    psum x1, blocking collectives, per_device(): lax.psum((query_part, key_part, value_part), 'seq')  139 us
    pmax x1, blocking collectives, per_device(): peak_target, peak_draft = lax.pmax((target_peak, draft_peak), 'seq')  135 us
    all_gather x1, blocking collectives, per_device(): lax.all_gather(projected.astype(jnp.bfloat16), 'head')  13.2 us
  transfers between devices with their start and end apart: 2, of which 2 were waited for; matrix products, arithmetic and copies ran while one was open for 1% of the time, Pallas kernels for 0%

profile of v1, /device:TPU:32, one launch (start us, length us, event | category | flops | bytes accessed | tf_op | source)
XLA Modules:
  0.0 623.6 jit_solution(7547033947280515958)
XLA Ops:
  7.3 0.9 copy.41
  8.2 1.2 convolution_bitcast_fusion
  12.8 144.7 %all-reduce.6.cloned.1.call-done = f32[8,5,8,128]{3,2,1,0:T(8,128)} async-done(((f32[8,5,8,128]{3,2,1,0:T(8,128)}), f32[8,5,8,128]{3,2,1,0:T(8,128)}) %all-reduce.6.cloned.1.call-update) | async-done | bytes 163856 | tf_op jit(solution)/shard_map/psum | solution.py:82
  157.5 1.1 subtract_convert_fusion
  158.7 0.9 select_reduce_fusion
  159.6 1.0 fusion.27
  160.9 1.0 fusion.30
  161.9 134.7 %all-reduce.2 = (f32[8,1,4,8]{3,2,0,1:T(4,128)}, f32[8,1,5,8]{3,2,0,1:T(8,128)S(1)}) all-reduce(f32[8,1,4,8]{3,2,0,1:T(4,128)} %bitcast.155, f32[8,1,5,8]{3,2,0,1:T(8,128)S(1)} %bitcast.153), channel_id=1, replica_groups=mesh['seq'=32,'head'=8] {'seq'}, use_global_device_ids=true, to_apply=%region_11.12 | all-reduce | flops 576 | bytes 4608 | tf_op jit(solution)/shard_map/pmax | solution.py:107
  296.6 1.4 bitcast_multiply_fusion
  298.0 1.4 bitcast_multiply_fusion.1
  299.4 138.9 %all-reduce = (f32[8,5,1,128]{3,1,0,2:T(8,128)}, f32[8,1,4,8]{3,2,0,1:T(4,128)}, bf16[40,128]{1,0:T(8,128)(2,1)}, f32[8,1,5,8]{3,2,0,1:T(8,128)}) all-reduce(f32[8,5,1,128]{3,1,0,2:T(8,128)} %reshape.256, f32[8,1,4,8]{3,2,0,1:T(4,128)} %get-tuple-element.33, f32[40,128]{1,0:T(8,128)} %fusion.88, ...), channel_id=1, replica_groups=mesh['seq'=32,'head'=8] {'seq'}, use_global_device_ids=true, to_apply=%region_4.5 | all-reduce | flops 10816 | bytes 76288 | tf_op jit(solution)/shard_map/psum | solution.py:82
  438.2 1.0 fusion.73
  439.3 1.4 fusion.66
  440.6 0.8 select_reduce_fusion.1
  442.0 2.0 fusion.47
  444.0 3.0 fusion.12
  447.1 1.2 fusion.20
  449.8 0.8 fusion.51
  450.6 0.8 fusion.78
  451.5 0.8 fusion.74
  452.3 147.3 %all-reduce.8.cloned.1.call-done = (f32[8,1,4,8,128]{4,3,2,0,1:T(8,128)}, f32[8,1,5,8,128]{4,3,2,0,1:T(8,128)}) async-done(((f32[8,1,4,8,128]{4,3,2,0,1:T(8,128)}, f32[8,1,5,8,128]{4,3,2,0,1:T(8,128)}), (f32[8,1,4,8,128]{4,3,2,0,1:T(8,128)}, f32[8,1,5,8,128]{4,3,2,0,1:T(8,128)})) %all-reduce.8.cloned.1.call-update) | async-done | bytes 294928 | tf_op jit(solution)/shard_map/psum | solution.py:110
  599.6 1.2 fusion.23
  600.9 1.1 fusion.26
  602.2 13.2 %all-gather = bf16[576,256]{1,0:T(8,128)(2,1)S(1)} all-gather(bf16[72,256]{1,0:T(8,128)(2,1)S(1)} %convolution_convert_fusion), channel_id=2, replica_groups=mesh['seq'=32,'head'=8] {'head'}, dimensions={0}, use_global_device_ids=true | all-gather | bytes 331776 | tf_op jit(solution)/shard_map/all_gather | solution.py:129
  (76 shorter events, 7.3 us)
Async XLA Ops:
  7.2 151.5 %copy-start = (bf16[8,1024,128]{2,1,0:T(8,128)(2,1)S(1)}, bf16[8,1024,128]{2,1,0:T(8,128)(2,1)}, u32[]{:S(2)}) copy-start(bf16[8,1024,128]{2,1,0:T(8,128)(2,1)} %param.14) | copy-start | bytes 6291460
  7.2 3.1 copy-start.19
  7.2 3.1 copy-start.17
  7.2 3.2 copy-start.11
  7.2 4.0 copy-start.12
  7.2 150.3 %all-reduce.6.cloned.1.call-start = ((), (), s32[]{:S(2)}) async-start(), calls=%async_computation | async-start | bytes 327680 | tf_op jit(solution)/shard_map/psum | solution.py:82
  10.1 589.5 %all-reduce.8.cloned.1.call-start = ((), (), s32[]{:S(2)}) async-start(), calls=%async_computation.1 | async-start | bytes 589824 | tf_op jit(solution)/shard_map/psum | solution.py:110
  10.2 148.5 %copy-start.18 = (f32[64]{0:T(128)}, f32[64]{0:T(128)S(1)}, u32[]{:S(2)}) copy-start(f32[64]{0:T(128)S(1)} %multiply_power_fusion) | copy-start | bytes 772
  10.2 1.7 copy-start.16
  10.3 148.4 %copy-start.13 = (f32[8,5]{1,0:T(8,128)}, f32[8,5]{1,0:T(8,128)S(1)}, u32[]{:S(2)}) copy-start(f32[8,5]{1,0:T(8,128)S(1)} %add_convert_fusion.1) | copy-start | bytes 484
  12.8 146.8 %copy-start.10 = (pred[8,1024]{1,0:T(8,128)(4,1)}, pred[8,1024]{1,0:T(8,128)(4,1)S(1)}, u32[]{:S(2)}) copy-start(pred[8,1024]{1,0:T(8,128)(4,1)S(1)} %get-tuple-element.35) | copy-start | bytes 24580
  12.8 148.0 %copy-start.8 = (pred[8,1024]{1,0:T(8,128)(4,1)}, pred[8,1024]{1,0:T(8,128)(4,1)S(1)}, u32[]{:S(2)}) copy-start(pred[8,1024]{1,0:T(8,128)(4,1)S(1)} %get-tuple-element.36) | copy-start | bytes 24580
  158.7 1.0 copy-start.1
  160.9 1.0 copy-start.5
  296.6 144.9 %copy-start.3 = (f32[8,1,5,8]{3,2,0,1:T(8,128)}, f32[8,1,5,8]{3,2,0,1:T(8,128)S(1)}, u32[]{:S(2)}) copy-start(f32[8,1,5,8]{3,2,0,1:T(8,128)S(1)} %get-tuple-element.17) | copy-start | bytes 3844
  441.4 0.6 copy-start.7
  444.0 3.0 copy-start.6
  444.0 3.0 copy-start.9
  444.0 3.0 copy-start.14
  444.0 3.0 copy-start.20
  447.0 4.4 copy-start.15
  447.0 4.4 copy-start.4
  450.6 151.4 %copy-start.2 = (bf16[1024,256]{1,0:T(8,128)(2,1)S(1)}, bf16[1024,256]{1,0:T(8,128)(2,1)}, u32[]{:S(2)}) copy-start(bf16[1024,256]{1,0:T(8,128)(2,1)} %param.13) | copy-start | bytes 1572868
Sparse Core Ops, SparseCore 0:
  11.5 146.0 all-reduce.5
  450.7 148.8 all-reduce.7
